TPU v7x, 32 devices: a whole 2x2x4 slice. The times are simulated.
32 devices in a mesh: row: 2 (over y), col: 16 (over z, x, core).
Axes of the slice: x: 2, y: 2, z: 4, core: 2. Of those that a mesh axis runs over, the one named last changes fastest.
Arguments:
- blocks: bfloat16 [128, 2048, 128], P('row', 'col'), may hold values from -0.1875 to 0.1875
- block_rows: int32 [2, 1024], P('row', 'col'), may hold values from 0 to 2047, as said below
- block_cols: int32 [2, 1024], P('row', 'col'), may hold values from 0 to 255
- counts: int32 [2, 16], P('row', 'col'), may hold values from 1 to 64, as said below
- start_vectors: float32 [32, 524288], P(None, ('row', 'col')), may hold values from -6 to 6
Outputs:
- vectors: float32 [32, 524288], P(None, ('row', 'col'))
Inputs may be any that keep to these rules, and one draw needn't show every extreme that they name: counts[r, c] is the number of live slots of grid position (r, c); in every draw some position has all 64 slots live. For every grid position (r, c) and every o < 16, exactly 4 of its 64 slots have block_rows[r, c * 64 + s] // 128 == o.
All inputs are finite; a program needn't handle non-finite values.
Results may differ from a plain program's by a relative error of at most 0.0036.
Values may be sent and summed in bfloat16 or wider, within the bound.
A program may use at most 256 MiB of HBM per device.

v0:
```python
import math
import jax
import jax.numpy as jnp
from jax import lax
from jax.sharding import PartitionSpec as P

N = 524288
ITERS = 2


def cholesky_lower(gram_matrix):
    matrix_order = gram_matrix.shape[0]
    positions = jnp.arange(matrix_order)

    def column_step(position, factor):
        before = (positions < position).astype(gram_matrix.dtype)
        target_row = lax.dynamic_index_in_dim(factor, position, 0, keepdims=False) * before
        column = lax.dynamic_index_in_dim(gram_matrix, position, 1, keepdims=False)
        residue = column - jnp.sum(factor * target_row[None, :], axis=1)
        on_diagonal = positions == position
        pivot_value = jnp.sqrt(jnp.sum(jnp.where(on_diagonal, residue, 0.0)))
        values = jnp.where(on_diagonal, pivot_value, residue / pivot_value)
        values = jnp.where(positions >= position, values, 0.0)
        return lax.dynamic_update_index_in_dim(factor, values, position, 1)

    return lax.fori_loop(0, matrix_order, column_step, jnp.zeros_like(gram_matrix))


def lower_inverse(lower_factor):
    matrix_order = lower_factor.shape[0]
    positions = jnp.arange(matrix_order)

    def row_step(position, inverse):
        lower_row = lax.dynamic_index_in_dim(lower_factor, position, 0, keepdims=False)
        before = (positions < position).astype(lower_factor.dtype)
        inner_sum = jnp.sum((lower_row * before)[:, None] * inverse, axis=0)
        unit_row = (positions == position).astype(lower_factor.dtype)
        pivot_value = jnp.sum(lower_row * unit_row)
        return lax.dynamic_update_index_in_dim(
            inverse, (unit_row - inner_sum) / pivot_value, position, 0
        )

    return lax.fori_loop(0, matrix_order, row_step, jnp.zeros_like(lower_factor))


def accumulate(blocks, rows_index, cols_index, live_count, row_panel, col_panel):
    slot_count, block_size = (blocks.shape[0], blocks.shape[1])
    vector_count = row_panel.shape[0]
    row_blocks = row_panel.reshape(vector_count, -1, block_size)
    col_blocks = col_panel.reshape(vector_count, -1, block_size)
    group_size = math.gcd(slot_count, 64)
    turn_count = (live_count + group_size - 1) // group_size
    slot_offsets = jnp.arange(group_size, dtype=jnp.int32)

    def one_group(turn_index, partial_sums):
        row_sums, col_sums = partial_sums
        first_slot = turn_index * group_size
        live_mask = (first_slot + slot_offsets < live_count).astype(jnp.float32)
        from_cols = jnp.take(col_blocks, cols_index, axis=1)
        from_rows = jnp.take(row_blocks, rows_index, axis=1)
        to_cols = jnp.einsum("kgi,gij->kgj", from_rows, blocks, preferred_element_type=jnp.float32)
        col_sums = col_sums.at[:, cols_index].add(to_cols * live_mask[None, :, None])
        to_rows = jnp.einsum("kgj,gij->kgi", from_cols, blocks, preferred_element_type=jnp.float32)
        row_sums = row_sums.at[:, rows_index].add(to_rows * live_mask[None, :, None])
        return (row_sums, col_sums)

    row_start = jnp.zeros(row_blocks.shape, jnp.float32)
    initial = (row_start, jnp.zeros(col_blocks.shape, jnp.float32))
    return lax.fori_loop(0, turn_count, one_group, initial)


def per_device(blocks, block_rows, block_cols, counts, start_vectors):
    live_count = counts[0, 0]
    rows_index = block_rows[0]
    cols_index = block_cols[0]
    vectors = start_vectors
    for iteration in range(ITERS):
        rounded = vectors.astype(jnp.bfloat16)
        vector_count = rounded.shape[0]
        col_panel = lax.all_gather(rounded, "row", axis=1, tiled=True)
        row_panel = lax.all_gather(rounded, "col", axis=1, tiled=True)
        row_sums, col_sums = accumulate(
            blocks, rows_index, cols_index, live_count, row_panel, col_panel
        )
        from_row_group = lax.psum_scatter(
            row_sums.reshape(vector_count, -1), "col", scatter_dimension=1, tiled=True
        )
        from_col_group = lax.psum_scatter(
            col_sums.reshape(vector_count, -1), "row", scatter_dimension=1, tiled=True
        )
        product = from_row_group + from_col_group
        local_gram = jnp.dot(
            product, product.T, precision=lax.Precision.HIGHEST, preferred_element_type=jnp.float32
        )
        gram_matrix = lax.psum(local_gram, ("row", "col")) / N
        inverse = lower_inverse(cholesky_lower(gram_matrix))
        vectors = jnp.dot(
            inverse, product, precision=lax.Precision.HIGHEST, preferred_element_type=jnp.float32
        )
    return vectors


def solution(mesh):
    placed = (
        P("row", "col", None),
        P("row", "col"),
        P("row", "col"),
        P("row", "col"),
        P(None, ("row", "col")),
    )
    return jax.shard_map(
        per_device, mesh=mesh, in_specs=placed, out_specs=P(None, ("row", "col")), check_vma=False
    )
```

profile of v0, /device:TPU:0, one launch (start us, length us, event | category | flops | bytes accessed | tf_op | source)
XLA Modules:
  0.0 1549.7 jit_solution(5209276909103308987)
XLA Ops:
  6.5 2.8 convert_element_type.66
  11.0 34.4 %all-gather.5.cloned.1.call-done = bf16[32,32768]{1,0:T(8,128)(2,1)} async-done(((bf16[32,16384]{1,0:T(8,128)(2,1)}), bf16[32,32768]{1,0:T(8,128)(2,1)}) %all-gather.5.cloned.1.call-update) | async-done | bytes 2097168 | tf_op jit(solution)/shard_map/all_gather | solution.py:80
  45.4 3.3 copy_bitcast_fusion.7
  48.6 2.2 gather_fusion
  50.9 2.2 fusion.34
  53.1 121.4 %all-gather.7.cloned.1.call-done = bf16[32,262144]{1,0:T(8,128)(2,1)} async-done(((bf16[32,16384]{1,0:T(8,128)(2,1)}), bf16[32,262144]{1,0:T(8,128)(2,1)}) %all-gather.7.cloned.1.call-update) | async-done | bytes 16777232 | tf_op jit(solution)/shard_map/all_gather | solution.py:81
  174.5 14.5 copy_bitcast_fusion.3
  189.0 6.4 gather_fusion.1
  195.4 1.7 fusion.32
  197.1 11.3 broadcast.314.clone
  208.4 2.6 broadcast.315.clone
  210.9 20.4 %while.90 = (s32[]{:T(128)}, f32[32,2048,128]{2,0,1:T(8,128)}, f32[32,256,128]{2,0,1:T(8,128)}, s32[]{:T(128)}, s32[64]{0:T(128)S(1)}, /*index=5*/s32[]{:T(128)}...) while((s32[]{:T(128)}, f32[32,2048,128]{2,0,1:T(8,128)}, ...), condition=%wide.region_3.6_spmd.clone, body=%wide.region_0.5_spmd.clone.sunk | while | flops 1049155 | bytes 10487937 | solution.py:69
  211.6 2.7 broadcast_multiply_fusion.8
  214.3 9.0 scatter_fusion
  223.3 8.0 scatter_fusion.1
  231.3 4.4 copy_bitcast_fusion.5
  235.8 22.6 %copy_bitcast_fusion.1 = f32[32,262144]{1,0:T(8,128)} fusion(f32[32,2048,128]{2,0,1:T(8,128)} %get-tuple-element.609), kind=kLoop, calls=%fused_computation.69 | loop fusion | bytes 67108864 | tf_op jit(solution)/shard_map/reshape | solution.py:86
  258.5 30.0 %reduce-scatter.7.cloned.1.call-done = f32[32,16384]{1,0:T(8,128)} async-done(((f32[32,32768]{1,0:T(8,128)}), f32[32,16384]{1,0:T(8,128)}) %reduce-scatter.7.cloned.1.call-update) | async-done | bytes 2097168 | tf_op jit(solution)/shard_map/reduce_scatter | solution.py:88
  288.4 337.4 %reduce-scatter.5.cloned.1.call-done = f32[32,16384]{1,0:T(8,128)} async-done(((f32[32,262144]{1,0:T(8,128)}), f32[32,16384]{1,0:T(8,128)}) %reduce-scatter.5.cloned.1.call-update) | async-done | bytes 2097168 | tf_op jit(solution)/shard_map/reduce_scatter | solution.py:85
  625.8 2.4 add.220
  629.5 1.8 fusion.52
  631.3 39.1 %psum.14 = f32[32,32]{1,0:T(8,128)S(1)} all-reduce(f32[32,32]{1,0:T(8,128)S(1)} %fusion.52), channel_id=1, replica_groups=mesh['row'=2,'col'=16] {'row','col'}, use_global_device_ids=true, to_apply=%region_6.9 | all-reduce | flops 1024 | bytes 8192 | tf_op jit(solution)/shard_map/psum | solution.py:95
  670.4 58.1 %while.92 = (s32[]{:T(128)}, f32[32,32]{1,0:T(8,128)S(1)}, f32[32,32]{0,1:T(8,128)S(1)}, s32[]{:T(128)}, s32[]{:T(128)}) while((s32[]{:T(128)}, f32[32,32]{1,0:T(8,128)S(1)}, f32[32,32]{0,1:T(8,128)S(1)}, s32[]{:T(128)}, s32[]{:T(128)}) %tuple.192), condition=%wide.region_10.13_spmd.clone.clone, body=%wide.region_7.12_spmd.clone.clone.sunk | while | flops 2401 | bytes 8913 | solution.py:26
  728.6 49.0 %while.93 = (s32[]{:T(128)}, f32[32,32]{1,0:T(8,128)S(1)}, f32[32,32]{1,0:T(8,128)S(1)}, s32[]{:T(128)}, s32[]{:T(128)}) while((s32[]{:T(128)}, f32[32,32]{1,0:T(8,128)S(1)}, f32[32,32]{1,0:T(8,128)S(1)}, s32[]{:T(128)}, s32[]{:T(128)}) %tuple.195), condition=%wide.region_14.17_spmd.clone.clone, body=%wide.region_11.16_spmd.clone.clone.sunk | while | flops 2305 | bytes 6221 | solution.py:43
  777.6 4.4 convolution_convert_fusion
  782.8 32.2 %all-gather.9.cloned.1.call-done = bf16[32,32768]{1,0:T(8,128)(2,1)} async-done(((bf16[32,16384]{1,0:T(8,128)(2,1)}), bf16[32,32768]{1,0:T(8,128)(2,1)}) %all-gather.9.cloned.1.call-update) | async-done | bytes 2097168 | tf_op jit(solution)/shard_map/all_gather | solution.py:80
  815.1 3.3 copy_bitcast_fusion.6
  818.3 2.2 gather_fusion.2
  820.6 2.2 fusion.30
  822.8 121.5 %all-gather.11.cloned.1.call-done = bf16[32,262144]{1,0:T(8,128)(2,1)} async-done(((bf16[32,16384]{1,0:T(8,128)(2,1)}), bf16[32,262144]{1,0:T(8,128)(2,1)}) %all-gather.11.cloned.1.call-update) | async-done | bytes 16777232 | tf_op jit(solution)/shard_map/all_gather | solution.py:81
  944.3 14.5 copy_bitcast_fusion.2
  958.8 6.4 gather_fusion.3
  966.9 11.3 broadcast.314
  978.2 2.6 broadcast.315
  980.7 20.4 %while.91 = (s32[]{:T(128)}, f32[32,2048,128]{2,0,1:T(8,128)}, f32[32,256,128]{2,0,1:T(8,128)}, s32[]{:T(128)}, s32[64]{0:T(128)S(1)}, /*index=5*/s32[]{:T(128)}...) while((s32[]{:T(128)}, f32[32,2048,128]{2,0,1:T(8,128)}, ...), condition=%wide.region_18.21_spmd.clone, body=%wide.region_15.20_spmd.clone.sunk | while | flops 1049155 | bytes 10487937 | solution.py:69
  981.4 2.7 broadcast_multiply_fusion.9
  984.1 9.0 scatter_fusion.2
  993.1 8.0 scatter_fusion.3
  1001.1 4.4 copy_bitcast_fusion.4
  1005.6 22.6 %copy_bitcast_fusion = f32[32,262144]{1,0:T(8,128)} fusion(f32[32,2048,128]{2,0,1:T(8,128)} %get-tuple-element.613), kind=kLoop, calls=%fused_computation.68 | loop fusion | bytes 67108864 | tf_op jit(solution)/shard_map/reshape | solution.py:86
  1028.2 30.0 %reduce-scatter.11.cloned.1.call-done = f32[32,16384]{1,0:T(8,128)} async-done(((f32[32,32768]{1,0:T(8,128)}), f32[32,16384]{1,0:T(8,128)}) %reduce-scatter.11.cloned.1.call-update) | async-done | bytes 2097168 | tf_op jit(solution)/shard_map/reduce_scatter | solution.py:88
  1058.2 336.9 %reduce-scatter.9.cloned.1.call-done = f32[32,16384]{1,0:T(8,128)} async-done(((f32[32,262144]{1,0:T(8,128)}), f32[32,16384]{1,0:T(8,128)}) %reduce-scatter.9.cloned.1.call-update) | async-done | bytes 2097168 | tf_op jit(solution)/shard_map/reduce_scatter | solution.py:85
  1395.2 2.4 add.221
  1398.9 1.8 fusion.53
  1400.7 39.0 %psum.15 = f32[32,32]{1,0:T(8,128)S(1)} all-reduce(f32[32,32]{1,0:T(8,128)S(1)} %fusion.53), channel_id=1, replica_groups=mesh['row'=2,'col'=16] {'row','col'}, use_global_device_ids=true, to_apply=%region_21.24 | all-reduce | flops 1024 | bytes 8192 | tf_op jit(solution)/shard_map/psum | solution.py:95
  1439.8 53.9 %while.94 = (s32[]{:T(128)}, f32[32,32]{1,0:T(8,128)S(1)}, f32[32,32]{0,1:T(8,128)S(1)}, s32[]{:T(128)}, s32[]{:T(128)}) while((s32[]{:T(128)}, f32[32,32]{1,0:T(8,128)S(1)}, f32[32,32]{0,1:T(8,128)S(1)}, s32[]{:T(128)}, s32[]{:T(128)}) %tuple.201), condition=%wide.region_25.28_spmd.clone.clone, body=%wide.region_22.27_spmd.clone.clone.sunk | while | flops 2401 | bytes 8913 | solution.py:26
  1493.7 44.3 %while.95 = (s32[]{:T(128)}, f32[32,32]{1,0:T(8,128)S(1)}, f32[32,32]{1,0:T(8,128)S(1)}, s32[]{:T(128)}, s32[]{:T(128)}) while((s32[]{:T(128)}, f32[32,32]{1,0:T(8,128)S(1)}, f32[32,32]{1,0:T(8,128)S(1)}, s32[]{:T(128)}, s32[]{:T(128)}) %tuple.204), condition=%wide.region_29.32_spmd.clone.clone, body=%wide.region_26.31_spmd.clone.clone.sunk | while | flops 2305 | bytes 6221 | solution.py:43
  1538.1 4.8 fusion.54
  (685 shorter events, 164.6 us)
Async XLA Ops:
  6.5 44.4 %copy-start = (bf16[64,128,128]{2,1,0:T(8,128)(2,1)S(1)}, bf16[64,128,128]{2,1,0:T(8,128)(2,1)}, u32[]{:S(2)}) copy-start(bf16[64,128,128]{2,1,0:T(8,128)(2,1)} %param.21) | copy-start | bytes 6291460
  6.5 4.3 copy-start.3
  6.5 4.4 copy-start.4
  6.5 38.8 %all-gather.5.cloned.1.call-start = ((), (), s32[]{:S(2)}) async-start(), calls=%async_computation.4 | async-start | bytes 3145728 | tf_op jit(solution)/shard_map/all_gather | solution.py:80
  9.4 165.1 %all-gather.7.cloned.1.call-start = ((), (), s32[]{:S(2)}) async-start(), calls=%async_computation.5 | async-start | bytes 17825792 | tf_op jit(solution)/shard_map/all_gather | solution.py:81
  10.2 278.3 %reduce-scatter.7.cloned.1.call-start = ((), (), s32[]{:S(2)}) async-start(), calls=%async_computation.7 | async-start | bytes 6291456 | tf_op jit(solution)/shard_map/reduce_scatter | solution.py:88
  235.8 390.0 %reduce-scatter.5.cloned.1.call-start = ((), (), s32[]{:S(2)}) async-start(), calls=%async_computation.6 | async-start | bytes 35651584 | tf_op jit(solution)/shard_map/reduce_scatter | solution.py:85
  258.4 556.7 %all-gather.9.cloned.1.call-start = ((), (), s32[]{:S(2)}) async-start(), calls=%async_computation.8 | async-start | bytes 3145728 | tf_op jit(solution)/shard_map/all_gather | solution.py:80
  628.2 1.3 copy-start.2
  782.0 162.3 %all-gather.11.cloned.1.call-start = ((), (), s32[]{:S(2)}) async-start(), calls=%async_computation.9 | async-start | bytes 17825792 | tf_op jit(solution)/shard_map/all_gather | solution.py:81
  782.6 275.6 %reduce-scatter.11.cloned.1.call-start = ((), (), s32[]{:S(2)}) async-start(), calls=%async_computation.11 | async-start | bytes 6291456 | tf_op jit(solution)/shard_map/reduce_scatter | solution.py:88
  1005.6 389.6 %reduce-scatter.9.cloned.1.call-start = ((), (), s32[]{:S(2)}) async-start(), calls=%async_computation.10 | async-start | bytes 35651584 | tf_op jit(solution)/shard_map/reduce_scatter | solution.py:85
  1397.6 1.4 copy-start.1
Sparse Core Ops, SparseCore 0:
  9.5 35.8 all-gather.4
  47.6 126.9 all-gather.6
  235.9 52.4 reduce-scatter.6
  293.1 332.6 reduce-scatter.4
  782.1 32.8 all-gather.8
  817.4 126.9 all-gather.10
  1005.7 52.4 reduce-scatter.10
  1062.5 332.6 reduce-scatter.8
where the time goes:
time: 1550 us
  waiting for transfers between devices  1050 us (68%)
  other arithmetic  189 us (12%)
  local copies, waits for them, and re-layouts  153 us (10%)
  blocking collectives  78.1 us (5%)
  loops' own time  48.3 us (3%)
  matrix products  20.5 us (1%)
    reduce_scatter x2, waiting for transfers between devices, per_device(): lax.psum_scatter(row_sums.reshape(vector_count, -1), 'col', scatter_dimen...  674 us
    all_gather x2, waiting for transfers between devices, per_device(): row_panel = lax.all_gather(rounded, 'col', axis=1, tiled=True)  243 us
    psum x2, blocking collectives, per_device(): gram_matrix = lax.psum(local_gram, ('row', 'col')) / N  78.1 us
    all_gather x2, waiting for transfers between devices, per_device(): col_panel = lax.all_gather(rounded, 'row', axis=1, tiled=True)  66.7 us
    reduce_scatter x2, waiting for transfers between devices, per_device(): lax.psum_scatter(col_sums.reshape(vector_count, -1), 'row', scatter_dimen...  60 us
    another operation x2, loops' own time, cholesky_lower(): lax.fori_loop(0, matrix_order, column_step, jnp.zeros_like(gram_matrix))  46.9 us
    reshape x2, local copies, waits for them, and re-layouts, per_device(): row_sums.reshape(vector_count, -1)  45.2 us
    reduce_sum x64, other arithmetic, column_step(): pivot_value = jnp.sqrt(jnp.sum(jnp.where(on_diagonal, residue, 0.0)))  42.8 us
  transfers between devices with their start and end apart: 8, of which 8 were waited for; matrix products, arithmetic and copies ran while one was open for 4% of the time, Pallas kernels for 0%

commit v1 on v0

--- a/solution.py
+++ b/solution.py
@@ -6,6 +6,18 @@
 
 N = 524288
 ITERS = 2
+
+
+def gather_by_bits(x, axis, dim):
+    ways, here, turn = (lax.axis_size(axis), lax.axis_index(axis), x.shape[dim])
+    line, have = (x, 1)
+    while have < ways:
+        line = jnp.concatenate(
+            [line, lax.ppermute(line, axis, [(d, (d - have) % ways) for d in range(ways)])],
+            axis=dim,
+        )
+        have = 2 * have
+    return jnp.roll(line, here * turn, axis=dim)
 
 
 def cholesky_lower(gram_matrix):
@@ -77,7 +89,7 @@
     for iteration in range(ITERS):
         rounded = vectors.astype(jnp.bfloat16)
         vector_count = rounded.shape[0]
-        col_panel = lax.all_gather(rounded, "row", axis=1, tiled=True)
+        col_panel = gather_by_bits(rounded, "row", 1)
         row_panel = lax.all_gather(rounded, "col", axis=1, tiled=True)
         row_sums, col_sums = accumulate(
             blocks, rows_index, cols_index, live_count, row_panel, col_panel

time: 1550 us -> 1480 us (0.955)
  waiting for transfers between devices: 1050 us -> 960 us
  other arithmetic: 189 us -> 205 us
    all_gather x2 -> x0, waiting for transfers between devices: 66.7 us -> none  [per_device(): col_panel = lax.all_gather(rounded, 'row', axis=1, tiled=True)]
    all_gather x2, waiting for transfers between devices: 243 us -> 181 us  [per_device(): row_panel = lax.all_gather(rounded, 'col', axis=1, tiled=True)]
    ppermute x0 -> x2, waiting for transfers between devices: none -> 44.6 us  [gather_by_bits(): lax.ppermute(line, axis, [(d, (d - have) % ways) for d in range(ways)])]
    reshape x0 -> x2, other arithmetic: none -> 15.9 us  [accumulate(): col_blocks = col_panel.reshape(vector_count, -1, block_size)]
  transfers between devices with their start and end apart: 8 -> 8, of which waited for: 8 -> 8; matrix products, arithmetic and copies ran while one was open for 4% -> 5% of each run, Pallas kernels for 0% -> 0%
where the time goes in v1:
time: 1480 us
  waiting for transfers between devices  960 us (65%)
  other arithmetic  205 us (14%)
  local copies, waits for them, and re-layouts  147 us (10%)
  blocking collectives  78.2 us (5%)
  loops' own time  48.3 us (3%)
  matrix products  20.5 us (1%)
    reduce_scatter x2, waiting for transfers between devices, per_device(): lax.psum_scatter(row_sums.reshape(vector_count, -1), 'col', scatter_dimen...  674 us
    all_gather x2, waiting for transfers between devices, per_device(): row_panel = lax.all_gather(rounded, 'col', axis=1, tiled=True)  181 us
    psum x2, blocking collectives, per_device(): gram_matrix = lax.psum(local_gram, ('row', 'col')) / N  78.2 us
    reduce_scatter x2, waiting for transfers between devices, per_device(): lax.psum_scatter(col_sums.reshape(vector_count, -1), 'row', scatter_dimen...  59.7 us
    another operation x2, loops' own time, cholesky_lower(): lax.fori_loop(0, matrix_order, column_step, jnp.zeros_like(gram_matrix))  46.9 us
    reshape x2, local copies, waits for them, and re-layouts, per_device(): row_sums.reshape(vector_count, -1)  45.2 us
    ppermute x2, waiting for transfers between devices, gather_by_bits(): lax.ppermute(line, axis, [(d, (d - have) % ways) for d in range(ways)])  44.6 us
    reduce_sum x64, other arithmetic, column_step(): pivot_value = jnp.sqrt(jnp.sum(jnp.where(on_diagonal, residue, 0.0)))  42.8 us
  transfers between devices with their start and end apart: 8, of which 8 were waited for; matrix products, arithmetic and copies ran while one was open for 5% of the time, Pallas kernels for 0%

profile of v1, /device:TPU:0, one launch (start us, length us, event | category | flops | bytes accessed | tf_op | source)
XLA Modules:
  0.0 1479.2 jit_solution(17562794134432505275)
XLA Ops:
  6.5 2.8 convert_element_type.66
  9.5 3.0 collective-permute-start
  13.3 22.6 %collective-permute-done = bf16[32,16384]{1,0:T(8,128)(2,1)S(1)} collective-permute-done((bf16[32,16384]{1,0:T(8,128)(2,1)}, bf16[32,16384]{1,0:T(8,128)(2,1)S(1)}, u32[]{:S(2)}, u32[]{:S(2)}) %collective-permute-start) | collective-permute-done | bytes 1048608 | tf_op jit(solution)/shard_map/ppermute | solution.py:16
  35.9 7.9 copy_bitcast_fusion.7
  43.8 2.3 gather_fusion
  46.1 2.2 fusion.42
  48.3 90.9 %all-gather.3.cloned.1.call-done = bf16[32,262144]{1,0:T(8,128)(2,1)} async-done(((bf16[32,16384]{1,0:T(8,128)(2,1)}), bf16[32,262144]{1,0:T(8,128)(2,1)}) %all-gather.3.cloned.1.call-update) | async-done | bytes 16777232 | tf_op jit(solution)/shard_map/all_gather | solution.py:93
  139.2 14.5 copy_bitcast_fusion.3
  153.7 6.4 gather_fusion.1
  161.8 11.3 broadcast.315.clone
  173.1 2.6 broadcast.316.clone
  175.6 20.4 %while.90 = (s32[]{:T(128)}, f32[32,2048,128]{2,0,1:T(8,128)}, f32[32,256,128]{2,0,1:T(8,128)}, s32[]{:T(128)}, s32[64]{0:T(128)S(1)}, /*index=5*/s32[]{:T(128)}...) while((s32[]{:T(128)}, f32[32,2048,128]{2,0,1:T(8,128)}, ...), condition=%wide.region_3.7_spmd.clone, body=%wide.region_0.6_spmd.clone.sunk | while | flops 1049155 | bytes 10487937 | solution.py:81
  176.3 2.7 broadcast_multiply_fusion.8
  179.0 9.0 scatter_fusion
  188.0 8.0 scatter_fusion.1
  196.0 4.4 copy_bitcast_fusion.5
  200.5 22.6 %copy_bitcast_fusion.1 = f32[32,262144]{1,0:T(8,128)} fusion(f32[32,2048,128]{2,0,1:T(8,128)} %get-tuple-element.610), kind=kLoop, calls=%fused_computation.69 | loop fusion | bytes 67108864 | tf_op jit(solution)/shard_map/reshape | solution.py:98
  223.2 30.0 %reduce-scatter.7.cloned.1.call-done = f32[32,16384]{1,0:T(8,128)} async-done(((f32[32,32768]{1,0:T(8,128)}), f32[32,16384]{1,0:T(8,128)}) %reduce-scatter.7.cloned.1.call-update) | async-done | bytes 2097168 | tf_op jit(solution)/shard_map/reduce_scatter | solution.py:100
  253.1 337.7 %reduce-scatter.5.cloned.1.call-done = f32[32,16384]{1,0:T(8,128)} async-done(((f32[32,262144]{1,0:T(8,128)}), f32[32,16384]{1,0:T(8,128)}) %reduce-scatter.5.cloned.1.call-update) | async-done | bytes 2097168 | tf_op jit(solution)/shard_map/reduce_scatter | solution.py:97
  590.8 2.4 add.228
  594.6 1.8 fusion.60
  596.3 39.2 %psum.14 = f32[32,32]{1,0:T(8,128)S(1)} all-reduce(f32[32,32]{1,0:T(8,128)S(1)} %fusion.60), channel_id=1, replica_groups=mesh['row'=2,'col'=16] {'row','col'}, use_global_device_ids=true, to_apply=%region_6.10 | all-reduce | flops 1024 | bytes 8192 | tf_op jit(solution)/shard_map/psum | solution.py:107
  635.6 58.1 %while.92 = (s32[]{:T(128)}, f32[32,32]{1,0:T(8,128)S(1)}, f32[32,32]{0,1:T(8,128)S(1)}, s32[]{:T(128)}, s32[]{:T(128)}) while((s32[]{:T(128)}, f32[32,32]{1,0:T(8,128)S(1)}, f32[32,32]{0,1:T(8,128)S(1)}, s32[]{:T(128)}, s32[]{:T(128)}) %tuple.194), condition=%wide.region_10.14_spmd.clone.clone, body=%wide.region_7.13_spmd.clone.clone.sunk | while | flops 2401 | bytes 8913 | solution.py:38
  693.7 48.9 %while.93 = (s32[]{:T(128)}, f32[32,32]{1,0:T(8,128)S(1)}, f32[32,32]{1,0:T(8,128)S(1)}, s32[]{:T(128)}, s32[]{:T(128)}) while((s32[]{:T(128)}, f32[32,32]{1,0:T(8,128)S(1)}, f32[32,32]{1,0:T(8,128)S(1)}, s32[]{:T(128)}, s32[]{:T(128)}) %tuple.197), condition=%wide.region_14.18_spmd.clone.clone, body=%wide.region_11.17_spmd.clone.clone.sunk | while | flops 2305 | bytes 6221 | solution.py:55
  742.7 4.4 convolution_convert_fusion
  747.2 2.4 collective-permute-start.1
  749.6 22.0 %collective-permute-done.1 = bf16[32,16384]{1,0:T(8,128)(2,1)S(1)} collective-permute-done((bf16[32,16384]{1,0:T(8,128)(2,1)}, bf16[32,16384]{1,0:T(8,128)(2,1)S(1)}, u32[]{:S(2)}, u32[]{:S(2)}) %collective-permute-start.1) | collective-permute-done | bytes 1048608 | tf_op jit(solution)/shard_map/ppermute | solution.py:16
  771.6 7.9 copy_bitcast_fusion.6
  779.5 2.2 gather_fusion.2
  781.8 2.2 fusion.38
  784.0 90.0 %all-gather.5.cloned.1.call-done = bf16[32,262144]{1,0:T(8,128)(2,1)} async-done(((bf16[32,16384]{1,0:T(8,128)(2,1)}), bf16[32,262144]{1,0:T(8,128)(2,1)}) %all-gather.5.cloned.1.call-update) | async-done | bytes 16777232 | tf_op jit(solution)/shard_map/all_gather | solution.py:93
  874.0 14.5 copy_bitcast_fusion.2
  888.5 6.4 gather_fusion.3
  896.6 11.3 broadcast.315
  907.9 2.6 broadcast.316
  910.4 20.4 %while.91 = (s32[]{:T(128)}, f32[32,2048,128]{2,0,1:T(8,128)}, f32[32,256,128]{2,0,1:T(8,128)}, s32[]{:T(128)}, s32[64]{0:T(128)S(1)}, /*index=5*/s32[]{:T(128)}...) while((s32[]{:T(128)}, f32[32,2048,128]{2,0,1:T(8,128)}, ...), condition=%wide.region_18.22_spmd.clone, body=%wide.region_15.21_spmd.clone.sunk | while | flops 1049155 | bytes 10487937 | solution.py:81
  911.1 2.7 broadcast_multiply_fusion.9
  913.8 9.0 scatter_fusion.2
  922.8 8.0 scatter_fusion.3
  930.8 4.4 copy_bitcast_fusion.4
  935.5 22.6 %copy_bitcast_fusion = f32[32,262144]{1,0:T(8,128)} fusion(f32[32,2048,128]{2,0,1:T(8,128)} %get-tuple-element.614), kind=kLoop, calls=%fused_computation.68 | loop fusion | bytes 67108864 | tf_op jit(solution)/shard_map/reshape | solution.py:98
  958.1 29.8 %reduce-scatter.11.cloned.1.call-done = f32[32,16384]{1,0:T(8,128)} async-done(((f32[32,32768]{1,0:T(8,128)}), f32[32,16384]{1,0:T(8,128)}) %reduce-scatter.11.cloned.1.call-update) | async-done | bytes 2097168 | tf_op jit(solution)/shard_map/reduce_scatter | solution.py:100
  987.9 336.8 %reduce-scatter.9.cloned.1.call-done = f32[32,16384]{1,0:T(8,128)} async-done(((f32[32,262144]{1,0:T(8,128)}), f32[32,16384]{1,0:T(8,128)}) %reduce-scatter.9.cloned.1.call-update) | async-done | bytes 2097168 | tf_op jit(solution)/shard_map/reduce_scatter | solution.py:97
  1324.7 2.4 add.229
  1330.3 39.0 %psum.15 = f32[32,32]{1,0:T(8,128)S(1)} all-reduce(f32[32,32]{1,0:T(8,128)S(1)} %fusion.61), channel_id=1, replica_groups=mesh['row'=2,'col'=16] {'row','col'}, use_global_device_ids=true, to_apply=%region_21.25 | all-reduce | flops 1024 | bytes 8192 | tf_op jit(solution)/shard_map/psum | solution.py:107
  1369.4 53.9 %while.94 = (s32[]{:T(128)}, f32[32,32]{1,0:T(8,128)S(1)}, f32[32,32]{0,1:T(8,128)S(1)}, s32[]{:T(128)}, s32[]{:T(128)}) while((s32[]{:T(128)}, f32[32,32]{1,0:T(8,128)S(1)}, f32[32,32]{0,1:T(8,128)S(1)}, s32[]{:T(128)}, s32[]{:T(128)}) %tuple.203), condition=%wide.region_25.29_spmd.clone.clone, body=%wide.region_22.28_spmd.clone.clone.sunk | while | flops 2401 | bytes 8913 | solution.py:38
  1423.3 44.3 %while.95 = (s32[]{:T(128)}, f32[32,32]{1,0:T(8,128)S(1)}, f32[32,32]{1,0:T(8,128)S(1)}, s32[]{:T(128)}, s32[]{:T(128)}) while((s32[]{:T(128)}, f32[32,32]{1,0:T(8,128)S(1)}, f32[32,32]{1,0:T(8,128)S(1)}, s32[]{:T(128)}, s32[]{:T(128)}) %tuple.206), condition=%wide.region_29.33_spmd.clone.clone, body=%wide.region_26.32_spmd.clone.clone.sunk | while | flops 2305 | bytes 6221 | solution.py:55
  1467.6 4.8 fusion.62
  (682 shorter events, 166.8 us)
Async XLA Ops:
  6.5 39.5 %copy-start = (bf16[64,128,128]{2,1,0:T(8,128)(2,1)S(1)}, bf16[64,128,128]{2,1,0:T(8,128)(2,1)}, u32[]{:S(2)}) copy-start(bf16[64,128,128]{2,1,0:T(8,128)(2,1)} %param.23) | copy-start | bytes 6291460
  6.5 6.6 copy-start.4
  6.5 6.7 copy-start.3
  6.5 132.7 %all-gather.3.cloned.1.call-start = ((), (), s32[]{:S(2)}) async-start(), calls=%async_computation.4 | async-start | bytes 17825792 | tf_op jit(solution)/shard_map/all_gather | solution.py:93
  9.4 243.7 %reduce-scatter.7.cloned.1.call-start = ((), (), s32[]{:S(2)}) async-start(), calls=%async_computation.6 | async-start | bytes 6291456 | tf_op jit(solution)/shard_map/reduce_scatter | solution.py:100
  9.5 26.4 %collective-permute-start = (bf16[32,16384]{1,0:T(8,128)(2,1)}, bf16[32,16384]{1,0:T(8,128)(2,1)S(1)}, u32[]{:S(2)}, u32[]{:S(2)}) collective-permute-start(bf16[32,16384]{1,0:T(8,128)(2,1)} %convert_element_type.66), channel_id=1, source_target_pairs={{0,16},{16,0},{1,17},{17,1},{2,18},{18,2},{3,19},{19,3},{4,20},{20... | collective-permute-start | bytes 3145736 | tf_op jit(solution)/shard_map/ppermute | solution.py:16
  200.5 390.3 %reduce-scatter.5.cloned.1.call-start = ((), (), s32[]{:S(2)}) async-start(), calls=%async_computation.5 | async-start | bytes 35651584 | tf_op jit(solution)/shard_map/reduce_scatter | solution.py:97
  223.1 650.9 %all-gather.5.cloned.1.call-start = ((), (), s32[]{:S(2)}) async-start(), calls=%async_computation.7 | async-start | bytes 17825792 | tf_op jit(solution)/shard_map/all_gather | solution.py:93
  593.2 1.3 copy-start.2
  747.2 240.8 %reduce-scatter.11.cloned.1.call-start = ((), (), s32[]{:S(2)}) async-start(), calls=%async_computation.9 | async-start | bytes 6291456 | tf_op jit(solution)/shard_map/reduce_scatter | solution.py:100
  747.2 24.4 %collective-permute-start.1 = (bf16[32,16384]{1,0:T(8,128)(2,1)}, bf16[32,16384]{1,0:T(8,128)(2,1)S(1)}, u32[]{:S(2)}, u32[]{:S(2)}) collective-permute-start(bf16[32,16384]{1,0:T(8,128)(2,1)} %convolution_convert_fusion), channel_id=1, source_target_pairs={{0,16},{16,0},{1,17},{17,1},{2,18},{18,2},{3,19},{19,3},{4,20},{20... | collective-permute-start | bytes 3145736 | tf_op jit(solution)/shard_map/ppermute | solution.py:16
  935.3 389.4 %reduce-scatter.9.cloned.1.call-start = ((), (), s32[]{:S(2)}) async-start(), calls=%async_computation.8 | async-start | bytes 35651584 | tf_op jit(solution)/shard_map/reduce_scatter | solution.py:97
  1327.1 1.4 copy-start.1
Sparse Core Ops, SparseCore 0:
  9.6 129.6 all-gather.2
  200.6 52.4 reduce-scatter.6
  258.0 332.7 reduce-scatter.4
  747.3 126.6 all-gather.4
  935.4 52.4 reduce-scatter.10
  992.0 332.6 reduce-scatter.8
